TPU v7x, 256 devices: a whole 4x4x8 slice. The times are simulated.
256 devices in a mesh: row: 8 (over x, y_hi), col: 32 (over y_lo, z, core).
Axes of the slice: x: 4, y: 4 (y_hi: 2, y_lo: 2; y = y_hi * 2 + y_lo), z: 8, core: 2. Of those that a mesh axis runs over, the one named last changes fastest.
Arguments:
- embed: float32 [65536, 128], P(('row', 'col')), may hold values from -6 to 6
- cotangent: float32 [65536, 128], P(('col', 'row')), may hold values from -6 to 6
- tile_values: float32 [32, 8, 128, 128, 128], P('col', 'row'), may hold values from 0 to 1
- tile_coords: int32 [2, 32, 8, 128], P(None, 'col', 'row'), may hold values from 0 to 63, as said below
- tile_count: int32 [32, 8], P('col', 'row'), may hold values from 1 to 128, as said below
- row_degree: int32 [65536], P(('col', 'row')), may hold values from 16 to 511
- col_degree: int32 [65536], P(('row', 'col')), may hold values from 16 to 511
Outputs:
- propagated: float32 [65536, 128], P(('col', 'row'))
- embed_grad: float32 [65536, 128], P(('row', 'col'))
Inputs may be any that keep to these rules, and one draw needn't show every extreme that they name: `tile_coords`: within one device block the slots hold distinct tile positions; the first component is below 16 and the second below 64. `tile_count`: some device block has all 128 slots live.
All inputs are finite; a program needn't handle non-finite values.
Results may differ from a plain program's by a relative error of at most 0.0003.
Values sent between devices are 32-bit elements; how exact they have to be, the bound alone decides.
A program may use at most 128 MiB of HBM per device.

v0:
```python
import jax
import jax.numpy as jnp
from jax import lax
from jax.sharding import PartitionSpec as P


def tile_terms(values, rows_at, cols_at, live_mask, panel_tiles, grad_tiles):
    picked = jnp.take(panel_tiles, cols_at, axis=0)
    forward_each = jnp.einsum("tij,tjd->tid", values, picked, precision=lax.Precision.HIGHEST)
    row_hot = (
        (rows_at[None, :] == jnp.arange(grad_tiles.shape[0], dtype=jnp.int32)[:, None])
        & live_mask[None, :]
    ).astype(jnp.float32)
    forward = jnp.einsum("at,tid->aid", row_hot, forward_each, precision=lax.Precision.HIGHEST)
    grad_picked = jnp.take(grad_tiles, rows_at, axis=0)
    backward_each = jnp.einsum("tij,tid->tjd", values, grad_picked, precision=lax.Precision.HIGHEST)
    col_hot = (
        (cols_at[None, :] == jnp.arange(panel_tiles.shape[0], dtype=jnp.int32)[:, None])
        & live_mask[None, :]
    ).astype(jnp.float32)
    backward = jnp.einsum("bt,tjd->bjd", col_hot, backward_each, precision=lax.Precision.HIGHEST)
    return (forward, backward)


def per_device(embed, cotangent, tile_values, tile_coords, tile_count, row_degree, col_degree):
    tile_size = tile_values.shape[-1]
    feature_width = embed.shape[1]
    capacity = tile_values.shape[2]
    values = tile_values[0, 0]
    rows_at = tile_coords[0, 0, 0]
    cols_at = tile_coords[1, 0, 0]
    live_count = tile_count[0, 0]
    scaled = embed * lax.rsqrt(col_degree.astype(jnp.float32))[:, None]
    grad_scaled = cotangent * lax.rsqrt(row_degree.astype(jnp.float32))[:, None]
    embed_panel = lax.all_gather(scaled, "col", axis=0, tiled=True)
    grad_panel = lax.all_gather(grad_scaled, "row", axis=0, tiled=True)
    panel_tiles = embed_panel.reshape(-1, tile_size, feature_width)
    grad_tiles = grad_panel.reshape(-1, tile_size, feature_width)
    live_mask = jnp.arange(capacity, dtype=jnp.int32) < live_count
    forward, backward = tile_terms(values, rows_at, cols_at, live_mask, panel_tiles, grad_tiles)
    summed = lax.psum_scatter(
        forward.reshape(-1, feature_width), "row", scatter_dimension=0, tiled=True
    )
    propagated = summed * lax.rsqrt(row_degree.astype(jnp.float32))[:, None]
    grad_summed = lax.psum_scatter(
        backward.reshape(-1, feature_width), "col", scatter_dimension=0, tiled=True
    )
    embed_grad = grad_summed * lax.rsqrt(col_degree.astype(jnp.float32))[:, None]
    return (propagated, embed_grad)


def solution(mesh):
    return jax.shard_map(
        per_device,
        mesh=mesh,
        in_specs=(
            P(("row", "col"), None),
            P(("col", "row"), None),
            P("col", "row", None, None, None),
            P(None, "col", "row", None),
            P("col", "row"),
            P(("col", "row")),
            P(("row", "col")),
        ),
        out_specs=(P(("col", "row"), None), P(("row", "col"), None)),
        check_vma=False,
    )
```

profile of v0, /device:TPU:2, one launch (start us, length us, event | category | flops | bytes accessed | tf_op | source)
XLA Modules:
  0.0 428.2 jit_solution(3082143181208052741)
XLA Ops:
  7.2 0.7 convert_rsqrt_fusion
  7.9 1.7 broadcast_multiply_fusion
  9.6 0.0 reduce-scatter.5.cloned.1.call-start
  10.3 0.7 fusion.25
  11.0 0.7 slice_bitcast_fusion
  11.7 0.7 compare_and_fusion
  12.3 53.9 %all-gather.5.cloned.1.call-done = f32[2048,128]{1,0:T(8,128)} async-done(((f32[256,128]{1,0:T(8,128)}), f32[2048,128]{1,0:T(8,128)}) %all-gather.5.cloned.1.call-update) | async-done | bytes 1048592 | tf_op jit(solution)/shard_map/all_gather | solution.py:36
  66.3 5.5 %gather_fusion.1 = f32[128,128,128]{2,1,0:T(8,128)} fusion(f32[16,128,128]{2,1,0:T(8,128)} %bitcast.39, s32[1024]{0:T(1024)S(1)} %pad_clamp_fusion), kind=kCustom, calls=%fused_computation.1 | custom fusion | bytes 16777728 | tf_op jit(solution)/shard_map/jit(_take)/gather | solution.py:15
  71.8 19.5 %fusion.4 = f32[128,128,128]{2,1,0:T(8,128)} fusion(f32[1,1,128,128,128]{4,3,2,1,0:T(8,128)} %param.9, f32[128,128,128]{2,1,0:T(8,128)} %gather_fusion.1, pred[128]{0:T(512)(128)(4,1)S(1)} %get-tuple-element.6), kind=kOutput, calls=%fused_computation.6 | convolution fusion | flops 3223322624 | bytes 25165952 | tf_op jit(solution)/shard_map/tij,tid->tjd/dot_general | solution.py:16
  91.2 9.4 %copy.12 = f32[128,128,128]{1,0,2:T(8,128)} copy(f32[128,128,128]{2,1,0:T(8,128)} %fusion.4) | data formatting | bytes 16777216 | tf_op jit(solution)/shard_map/tij,tid->tjd/dot_general | solution.py:16
  100.6 6.0 %fusion = f32[64,128,128]{2,0,1:T(8,128)S(1)} fusion(f32[128,128,128]{1,0,2:T(8,128)} %copy.12, s32[128]{0:T(128)S(1)} %get-tuple-element.4, pred[128]{0:T(512)(128)(4,1)S(1)} %iota_compare_fusion.2), kind=kOutput, calls=%fused_computation.2 | convolution fusion | flops 1610629120 | bytes 12583552 | tf_op jit(solution)/shard_map/bt,tjd->bjd/dot_general | solution.py:21
  106.7 4.4 %copy.10 = f32[64,128,128]{2,1,0:T(8,128)} copy(f32[64,128,128]{2,0,1:T(8,128)S(1)} %fusion) | data formatting | bytes 8388608 | tf_op jit(solution)/shard_map/bt,tjd->bjd/dot_general | solution.py:21
  111.1 0.0 all-gather.3.cloned.1.call-start
  111.1 122.8 %reduce-scatter.5.cloned.1.call-done = f32[256,128]{1,0:T(8,128)} async-done(((f32[8192,128]{1,0:T(8,128)}), f32[256,128]{1,0:T(8,128)}) %reduce-scatter.5.cloned.1.call-update) | async-done | bytes 131088 | tf_op jit(solution)/shard_map/reduce_scatter | solution.py:45
  233.9 1.7 broadcast_multiply_fusion.2
  235.7 0.0 reduce-scatter.3.cloned.1.call-start
  235.7 62.9 %all-gather.3.cloned.1.call-done = f32[8192,128]{1,0:T(8,128)} async-done(((f32[256,128]{1,0:T(8,128)}), f32[8192,128]{1,0:T(8,128)}) %all-gather.3.cloned.1.call-update) | async-done | bytes 4194320 | tf_op jit(solution)/shard_map/all_gather | solution.py:35
  298.6 6.5 %gather_fusion = f32[128,128,128]{2,1,0:T(8,128)} fusion(f32[64,128,128]{2,1,0:T(8,128)} %bitcast.40, s32[1024]{0:T(1024)S(1)} %pad_clamp_fusion.1), kind=kCustom, calls=%fused_computation | custom fusion | bytes 16777728 | tf_op jit(solution)/shard_map/jit(_take)/gather | solution.py:8
  305.1 21.2 %fusion.6 = f32[128,128,128]{2,1,0:T(8,128)} fusion(f32[1,1,128,128,128]{4,3,2,1,0:T(8,128)} %param.9, f32[128,128,128]{2,1,0:T(8,128)} %gather_fusion, pred[128]{0:T(512)(128)(4,1)S(1)} %get-tuple-element.7), kind=kOutput, calls=%fused_computation.8 | convolution fusion | flops 3223322624 | bytes 25165952 | tf_op jit(solution)/shard_map/tij,tjd->tid/dot_general | solution.py:9
  326.3 9.4 %copy.11 = f32[128,128,128]{1,0,2:T(8,128)} copy(f32[128,128,128]{2,1,0:T(8,128)} %fusion.6) | data formatting | bytes 16777216 | tf_op jit(solution)/shard_map/tij,tjd->tid/dot_general | solution.py:9
  335.6 5.2 %fusion.2 = f32[16,128,128]{2,0,1:T(8,128)S(1)} fusion(f32[128,128,128]{1,0,2:T(8,128)} %copy.11, s32[128]{0:T(128)S(1)} %get-tuple-element.5, pred[128]{0:T(512)(128)(4,1)S(1)} %iota_compare_fusion.2), kind=kOutput, calls=%fused_computation.4 | convolution fusion | flops 402657280 | bytes 9437824 | tf_op jit(solution)/shard_map/at,tid->aid/dot_general | solution.py:14
  340.8 1.3 copy.9
  342.1 77.9 %reduce-scatter.3.cloned.1.call-done = f32[256,128]{1,0:T(8,128)} async-done(((f32[2048,128]{1,0:T(8,128)}), f32[256,128]{1,0:T(8,128)}) %reduce-scatter.3.cloned.1.call-update) | async-done | bytes 131088 | tf_op jit(solution)/shard_map/reduce_scatter | solution.py:41
  420.0 1.7 broadcast_multiply_fusion.1
  (13 shorter events, 0.1 us)
Async XLA Ops:
  7.2 59.1 %all-gather.5.cloned.1.call-start = ((), (), s32[]{:S(2)}) async-start(), calls=%async_computation.4 | async-start | bytes 1179648 | tf_op jit(solution)/shard_map/all_gather | solution.py:36
  9.6 224.4 %reduce-scatter.5.cloned.1.call-start = ((), (), s32[]{:S(2)}) async-start(), calls=%async_computation.5 | async-start | bytes 4325376 | tf_op jit(solution)/shard_map/reduce_scatter | solution.py:45
  106.6 4.5 %copy-start.1 = (s32[256]{0:T(256)S(1)}, s32[256]{0:T(256)}, u32[]{:S(2)}) copy-start(s32[256]{0:T(256)} %param.13) | copy-start | bytes 3076
  106.6 127.3 %copy-start = (f32[256,128]{1,0:T(8,128)S(1)}, f32[256,128]{1,0:T(8,128)}, u32[]{:S(2)}) copy-start(f32[256,128]{1,0:T(8,128)} %param.7) | copy-start | bytes 393220
  111.1 187.5 %all-gather.3.cloned.1.call-start = ((), (), s32[]{:S(2)}) async-start(), calls=%async_computation.2 | async-start | bytes 4325376 | tf_op jit(solution)/shard_map/all_gather | solution.py:35
  235.7 184.3 %reduce-scatter.3.cloned.1.call-start = ((), (), s32[]{:S(2)}) async-start(), calls=%async_computation.3 | async-start | bytes 1179648 | tf_op jit(solution)/shard_map/reduce_scatter | solution.py:41
Sparse Core Ops, SparseCore 0:
  11.2 55.0 all-gather.4
  111.2 122.7 reduce-scatter.4
  236.4 62.1 all-gather.2
  342.2 77.7 reduce-scatter.2
where the time goes:
time: 429 us; the launch traced here: 428 us
  waiting for transfers between devices  318 us (74%)
  matrix products  51.9 us (12%)
  local copies, waits for them, and re-layouts  37.1 us (9%)
  between operations  14.5 us (3%)
  other arithmetic  7.09 us (2%)
    reduce_scatter x1, waiting for transfers between devices, per_device(): lax.psum_scatter(backward.reshape(-1, feature_width), 'col', scatter_dime...  123 us
    reduce_scatter x1, waiting for transfers between devices, per_device(): lax.psum_scatter(forward.reshape(-1, feature_width), 'row', scatter_dimen...  77.9 us
    all_gather x1, waiting for transfers between devices, per_device(): embed_panel = lax.all_gather(scaled, 'col', axis=0, tiled=True)  62.9 us
    all_gather x1, waiting for transfers between devices, per_device(): grad_panel = lax.all_gather(grad_scaled, 'row', axis=0, tiled=True)  53.9 us
    dot_general x1, matrix products, tile_terms(): jnp.einsum('tij,tjd->tid', values, picked, precision=lax.Precision.HIGHEST)  21.2 us
    dot_general x1, matrix products, tile_terms(): jnp.einsum('tij,tid->tjd', values, grad_picked, precision=lax.Precision.H...  19.5 us
    dot_general x1, local copies, waits for them, and re-layouts, tile_terms(): jnp.einsum('tij,tid->tjd', values, grad_picked, precision=lax.Precision.H...  9.36 us
    dot_general x1, local copies, waits for them, and re-layouts, tile_terms(): jnp.einsum('tij,tjd->tid', values, picked, precision=lax.Precision.HIGHEST)  9.36 us
  transfers between devices with their start and end apart: 4, of which 4 were waited for; matrix products, arithmetic and copies ran while one was open for 0% of the time, Pallas kernels for 0%

commit v1 on v0

--- a/solution.py
+++ b/solution.py
@@ -33,7 +33,10 @@
     scaled = embed * lax.rsqrt(col_degree.astype(jnp.float32))[:, None]
     grad_scaled = cotangent * lax.rsqrt(row_degree.astype(jnp.float32))[:, None]
     embed_panel = lax.all_gather(scaled, "col", axis=0, tiled=True)
-    grad_panel = lax.all_gather(grad_scaled, "row", axis=0, tiled=True)
+    devices = lax.axis_size("row")
+    blocks = jnp.stack([grad_scaled for _ in range(devices)])
+    blocks = lax.all_to_all(blocks, "row", split_axis=0, concat_axis=0)
+    grad_panel = jnp.concatenate(blocks, axis=0)
     panel_tiles = embed_panel.reshape(-1, tile_size, feature_width)
     grad_tiles = grad_panel.reshape(-1, tile_size, feature_width)
     live_mask = jnp.arange(capacity, dtype=jnp.int32) < live_count

time: 429 us -> 395 us (0.921)
  waiting for transfers between devices: 318 us -> 278 us
  starting transfers between devices: 0.16 us -> 7.55 us
    all_gather x1 -> x0, waiting for transfers between devices: 53.9 us -> none  [per_device(): grad_panel = lax.all_gather(grad_scaled, 'row', axis=0, tiled=True)]
    all_to_all x0 -> x1, waiting for transfers between devices: none -> 11.8 us  [per_device(): blocks = lax.all_to_all(blocks, 'row', split_axis=0, concat_axis=0)]
    all_to_all x0 -> x1, starting transfers between devices: none -> 7.46 us  [per_device(): blocks = lax.all_to_all(blocks, 'row', split_axis=0, concat_axis=0)]
  transfers between devices with their start and end apart: 4 -> 4, of which waited for: 4 -> 4; matrix products, arithmetic and copies ran while one was open for 0% -> 1% of each run, Pallas kernels for 0% -> 0%
where the time goes in v1:
time: 395 us
  waiting for transfers between devices  278 us (70%)
  matrix products  51.9 us (13%)
  local copies, waits for them, and re-layouts  36.8 us (9%)
  between operations  14.5 us (4%)
  starting transfers between devices  7.55 us (2%)
  other arithmetic  6.43 us (2%)
    reduce_scatter x1, waiting for transfers between devices, per_device(): lax.psum_scatter(backward.reshape(-1, feature_width), 'col', scatter_dime...  125 us
    reduce_scatter x1, waiting for transfers between devices, per_device(): lax.psum_scatter(forward.reshape(-1, feature_width), 'row', scatter_dimen...  77.8 us
    all_gather x1, waiting for transfers between devices, per_device(): embed_panel = lax.all_gather(scaled, 'col', axis=0, tiled=True)  63.3 us
    dot_general x1, matrix products, tile_terms(): jnp.einsum('tij,tjd->tid', values, picked, precision=lax.Precision.HIGHEST)  21.2 us
    dot_general x1, matrix products, tile_terms(): jnp.einsum('tij,tid->tjd', values, grad_picked, precision=lax.Precision.H...  19.5 us
    all_to_all x1, waiting for transfers between devices, per_device(): blocks = lax.all_to_all(blocks, 'row', split_axis=0, concat_axis=0)  11.8 us
    dot_general x1, local copies, waits for them, and re-layouts, tile_terms(): jnp.einsum('tij,tjd->tid', values, picked, precision=lax.Precision.HIGHEST)  9.31 us
    dot_general x1, local copies, waits for them, and re-layouts, tile_terms(): jnp.einsum('tij,tid->tjd', values, grad_picked, precision=lax.Precision.H...  9.26 us
  transfers between devices with their start and end apart: 4, of which 4 were waited for; matrix products, arithmetic and copies ran while one was open for 1% of the time, Pallas kernels for 0%

profile of v1, /device:TPU:2, one launch (start us, length us, event | category | flops | bytes accessed | tf_op | source)
XLA Modules:
  0.0 394.7 jit_solution(3444113678193743025)
XLA Ops:
  7.2 0.7 convert_rsqrt_fusion
  7.8 1.0 broadcast_multiply_fusion
  8.9 1.0 stack.2
  9.9 7.5 %all-to-all-start = ((f32[8,256,128]{2,1,0:T(8,128)}), f32[8,256,128]{2,1,0:T(8,128)S(1)}, u32[]{:S(2)}, u32[]{:S(2)}) async-start(f32[8,256,128]{2,1,0:T(8,128)} %stack.2), calls=%async_computation.1 | async-start | bytes 2097152 | tf_op jit(solution)/shard_map/all_to_all | solution.py:38
  18.0 0.7 fusion.25
  18.7 0.7 slice_bitcast_fusion
  19.4 0.7 compare_and_fusion
  20.1 11.8 %all-to-all-done = f32[8,256,128]{2,1,0:T(8,128)S(1)} async-done(((f32[8,256,128]{2,1,0:T(8,128)}), f32[8,256,128]{2,1,0:T(8,128)S(1)}, u32[]{:S(2)}, u32[]{:S(2)}) %all-to-all-start) | async-done | bytes 1048608 | tf_op jit(solution)/shard_map/all_to_all | solution.py:38
  31.9 4.3 %gather_fusion.1 = f32[128,128,128]{2,1,0:T(8,128)} fusion(f32[16,128,128]{2,1,0:T(8,128)S(1)} %bitcast.39, s32[1024]{0:T(1024)S(1)} %pad_clamp_fusion), kind=kCustom, calls=%fused_computation.1 | custom fusion | bytes 16777728 | tf_op jit(solution)/shard_map/jit(_take)/gather | solution.py:15
  36.2 19.5 %fusion.4 = f32[128,128,128]{2,1,0:T(8,128)} fusion(f32[1,1,128,128,128]{4,3,2,1,0:T(8,128)} %param.9, f32[128,128,128]{2,1,0:T(8,128)} %gather_fusion.1, pred[128]{0:T(512)(128)(4,1)S(1)} %get-tuple-element.6), kind=kOutput, calls=%fused_computation.6 | convolution fusion | flops 3223322624 | bytes 25165952 | tf_op jit(solution)/shard_map/tij,tid->tjd/dot_general | solution.py:16
  55.7 9.3 %copy.12 = f32[128,128,128]{1,0,2:T(8,128)} copy(f32[128,128,128]{2,1,0:T(8,128)} %fusion.4) | data formatting | bytes 16777216 | tf_op jit(solution)/shard_map/tij,tid->tjd/dot_general | solution.py:16
  65.0 6.0 %fusion = f32[64,128,128]{2,0,1:T(8,128)S(1)} fusion(f32[128,128,128]{1,0,2:T(8,128)} %copy.12, s32[128]{0:T(128)S(1)} %get-tuple-element.4, pred[128]{0:T(512)(128)(4,1)S(1)} %iota_compare_fusion.2), kind=kOutput, calls=%fused_computation.2 | convolution fusion | flops 1610629120 | bytes 12583552 | tf_op jit(solution)/shard_map/bt,tjd->bjd/dot_general | solution.py:21
  71.1 4.4 %copy.10 = f32[64,128,128]{2,1,0:T(8,128)} copy(f32[64,128,128]{2,0,1:T(8,128)S(1)} %fusion) | data formatting | bytes 8388608 | tf_op jit(solution)/shard_map/bt,tjd->bjd/dot_general | solution.py:21
  75.5 0.0 all-gather.2.cloned.1.call-start
  75.5 124.6 %reduce-scatter.5.cloned.1.call-done = f32[256,128]{1,0:T(8,128)} async-done(((f32[8192,128]{1,0:T(8,128)}), f32[256,128]{1,0:T(8,128)}) %reduce-scatter.5.cloned.1.call-update) | async-done | bytes 131088 | tf_op jit(solution)/shard_map/reduce_scatter | solution.py:48
  200.1 1.7 broadcast_multiply_fusion.2
  201.9 63.3 %all-gather.2.cloned.1.call-done = f32[8192,128]{1,0:T(8,128)} async-done(((f32[256,128]{1,0:T(8,128)}), f32[8192,128]{1,0:T(8,128)}) %all-gather.2.cloned.1.call-update) | async-done | bytes 4194320 | tf_op jit(solution)/shard_map/all_gather | solution.py:35
  265.2 6.5 %gather_fusion = f32[128,128,128]{2,1,0:T(8,128)} fusion(f32[64,128,128]{2,1,0:T(8,128)} %bitcast.40, s32[1024]{0:T(1024)S(1)} %pad_clamp_fusion.1), kind=kCustom, calls=%fused_computation | custom fusion | bytes 16777728 | tf_op jit(solution)/shard_map/jit(_take)/gather | solution.py:8
  271.7 21.2 %fusion.6 = f32[128,128,128]{2,1,0:T(8,128)} fusion(f32[1,1,128,128,128]{4,3,2,1,0:T(8,128)} %param.9, f32[128,128,128]{2,1,0:T(8,128)} %gather_fusion, pred[128]{0:T(512)(128)(4,1)S(1)} %get-tuple-element.7), kind=kOutput, calls=%fused_computation.8 | convolution fusion | flops 3223322624 | bytes 25165952 | tf_op jit(solution)/shard_map/tij,tjd->tid/dot_general | solution.py:9
  292.9 9.3 %copy.11 = f32[128,128,128]{1,0,2:T(8,128)} copy(f32[128,128,128]{2,1,0:T(8,128)} %fusion.6) | data formatting | bytes 16777216 | tf_op jit(solution)/shard_map/tij,tjd->tid/dot_general | solution.py:9
  302.2 5.2 %fusion.2 = f32[16,128,128]{2,0,1:T(8,128)S(1)} fusion(f32[128,128,128]{1,0,2:T(8,128)} %copy.11, s32[128]{0:T(128)S(1)} %get-tuple-element.5, pred[128]{0:T(512)(128)(4,1)S(1)} %iota_compare_fusion.2), kind=kOutput, calls=%fused_computation.4 | convolution fusion | flops 402657280 | bytes 9437824 | tf_op jit(solution)/shard_map/at,tid->aid/dot_general | solution.py:14
  307.4 1.3 copy.9
  308.7 77.8 %reduce-scatter.3.cloned.1.call-done = f32[256,128]{1,0:T(8,128)} async-done(((f32[2048,128]{1,0:T(8,128)}), f32[256,128]{1,0:T(8,128)}) %reduce-scatter.3.cloned.1.call-update) | async-done | bytes 131088 | tf_op jit(solution)/shard_map/reduce_scatter | solution.py:44
  386.5 1.7 broadcast_multiply_fusion.1
  (13 shorter events, 0.1 us)
Async XLA Ops:
  9.9 22.0 %all-to-all-start = ((f32[8,256,128]{2,1,0:T(8,128)}), f32[8,256,128]{2,1,0:T(8,128)S(1)}, u32[]{:S(2)}, u32[]{:S(2)}) async-start(f32[8,256,128]{2,1,0:T(8,128)} %stack.2), calls=%async_computation.1 | async-start | bytes 2097152 | tf_op jit(solution)/shard_map/all_to_all | solution.py:38
  17.4 182.8 %reduce-scatter.5.cloned.1.call-start = ((), (), s32[]{:S(2)}) async-start(), calls=%async_computation.5 | async-start | bytes 4325376 | tf_op jit(solution)/shard_map/reduce_scatter | solution.py:48
  71.0 4.5 %copy-start.1 = (s32[256]{0:T(256)S(1)}, s32[256]{0:T(256)}, u32[]{:S(2)}) copy-start(s32[256]{0:T(256)} %param.13) | copy-start | bytes 3076
  71.0 129.1 %copy-start = (f32[256,128]{1,0:T(8,128)S(1)}, f32[256,128]{1,0:T(8,128)}, u32[]{:S(2)}) copy-start(f32[256,128]{1,0:T(8,128)} %param.7) | copy-start | bytes 393220
  75.5 189.7 %all-gather.2.cloned.1.call-start = ((), (), s32[]{:S(2)}) async-start(), calls=%async_computation.3 | async-start | bytes 4325376 | tf_op jit(solution)/shard_map/all_gather | solution.py:35
  201.9 184.7 %reduce-scatter.3.cloned.1.call-start = ((), (), s32[]{:S(2)}) async-start(), calls=%async_computation.4 | async-start | bytes 1179648 | tf_op jit(solution)/shard_map/reduce_scatter | solution.py:44
Sparse Core Ops, SparseCore 0:
  75.6 124.5 reduce-scatter.4
  202.6 62.5 all-gather.1
  308.8 77.6 reduce-scatter.2
